TPU v7x, 128 devices: a whole 4x4x4 slice. The times are simulated.
128 devices in a mesh: prow: 8 (over y_lo, z), pcol: 16 (over x, y_hi, core).
Axes of the slice: x: 4, y: 4 (y_hi: 2, y_lo: 2; y = y_hi * 2 + y_lo), z: 4, core: 2. Of those that a mesh axis runs over, the one named last changes fastest.
Arguments:
- anc_inverse: float32 [4096, 4096], P('pcol', 'prow')
- pattern_one: int32 [16, 8], replicated, may hold values from 0 to 15, as said below
- parents: int32 [16], replicated, may hold values from 0 to 15, as said below
- low_one: float32 [16, 2048, 256], P('pcol', 'prow'), may hold values from -2 to 2
- pivot_one: float32 [16, 256, 256], P('pcol'), may hold values from -4 to 4
- low_two: float32 [16, 2048, 256], P('pcol', 'prow'), may hold values from -2 to 2
- second_scaled_factor: float32 [16, 256, 256], P('pcol'), may hold values from -2 to 2
- second_pivot_inverse: float32 [16, 256, 256], P('pcol'), may hold values from -4 to 4
Outputs:
- column_one: float32 [16, 4096, 256], P('prow', 'pcol')
- diag_one: float32 [16, 256, 256], P('pcol')
- column_two: float32 [16, 4096, 256], P('prow', 'pcol')
- second_parent_inverse: float32 [16, 256, 256], P('pcol')
- second_diagonal_inverse: float32 [16, 256, 256], P('pcol')
Inputs may be any that keep to these rules, and one draw needn't show every extreme that they name: `pattern_one`: entry r of each row names an ancestor of process row r: it lies in r * 2 to r * 2 + 1; for each r, every ancestor of that range is entry r of exactly 8 rows. `parents`: every first-level supernode is the parent of exactly one second-level supernode.
All inputs are finite; a program needn't handle non-finite values.
Results may differ from a plain program's by a relative error of at most 0.000073.
Values sent between devices are 32-bit elements; how exact they have to be, the bound alone decides.
No kernel may reach another device: no remote copies, remote signals or barrier semaphores. Data moves between devices by JAX's collectives and lax.ppermute only.
A program may use at most 128 MiB of HBM per device.

v0:
```python
import jax
import jax.numpy as jnp
from jax import lax
from jax.sharding import PartitionSpec as P


def in_one_piece(arrays, axis, dim, along):
    widths = [a.shape[along] for a in arrays]
    both = jnp.concatenate(arrays, axis=along)
    result = lax.all_gather(both, axis, axis=dim, tiled=True)
    return tuple(jnp.split(result, [sum(widths[:k]) for k in range(1, len(widths))], axis=along))


def sent_to_all(x, axis):
    copies = jnp.broadcast_to(x, (lax.axis_size(axis), *x.shape))
    return lax.all_to_all(copies, axis, split_axis=0, concat_axis=0, tiled=True)


def over_copies(x, axis):
    return sent_to_all(x, axis).sum(axis=0)


def side_by_side(arrays, axis, dim, along):
    both = jnp.concatenate(arrays, axis=along)
    result, at, outs = (lax.psum_scatter(both, axis, scatter_dimension=dim, tiled=True), 0, [])
    for a in arrays:
        outs.append(lax.slice_in_dim(result, at, at + a.shape[along], axis=along))
        at += a.shape[along]
    return tuple(outs)


def together(arrays, axis):
    line, at, outs = (jnp.concatenate([a.reshape(-1) for a in arrays]), 0, [])
    subtotal = over_copies(line, axis)
    for a in arrays:
        outs.append(subtotal[at : at + a.size].reshape(a.shape))
        at += a.size
    return tuple(outs)


def batched(left, right):
    return jnp.einsum("kab,kbd->kad", left, right, precision=lax.Precision.HIGHEST)


def batched_left_t(left, right):
    return jnp.einsum("kba,kbd->kad", left, right, precision=lax.Precision.HIGHEST)


def pick_rows(hit_mask, count):
    total = hit_mask.shape[0]
    keys = jnp.where(hit_mask, 0, total).astype(jnp.int32) + jnp.arange(total, dtype=jnp.int32)
    chosen_rows = jnp.argsort(keys)[:count]
    valid = jnp.take(hit_mask, chosen_rows, axis=0).astype(jnp.float32)[:, None, None]
    return (chosen_rows, valid)


def body(
    anc_inverse,
    pattern_one,
    parents,
    low_one,
    pivot_one,
    low_two,
    second_scaled_factor,
    second_pivot_inverse,
):
    my_row = lax.axis_index("prow")
    my_col = lax.axis_index("pcol")
    row_count = lax.axis_size("prow")
    col_count = lax.axis_size("pcol")
    per_row_anc = col_count // row_count
    supernode_block_width = pivot_one.shape[1]
    per_col_one = pivot_one.shape[0]
    per_col_two = second_scaled_factor.shape[0]
    owned = anc_inverse.shape[1] // supernode_block_width
    zblocks = anc_inverse.reshape(supernode_block_width, owned, supernode_block_width).transpose(
        1, 0, 2
    )
    lowall = lax.all_gather(low_one, "pcol", axis=0, tiled=True)
    total_one = lowall.shape[0]
    owned_slot_list = lax.dynamic_index_in_dim(pattern_one, my_row, 1, keepdims=False)
    chosen = jnp.take(zblocks, owned_slot_list - my_row * owned, axis=0)
    first_terms = batched(chosen, lowall)
    lowsec, topall = in_one_piece((low_two, second_scaled_factor), "pcol", 0, 1)
    total_two = lowsec.shape[0]
    pattern_two = jnp.take(pattern_one, parents, axis=0)
    my_slots_two = lax.dynamic_index_in_dim(pattern_two, my_row, 1, keepdims=False)
    chosen_two = jnp.take(zblocks, my_slots_two - my_row * owned, axis=0)
    first_full = -lax.psum(first_terms, "prow")
    share = total_two // row_count
    start = my_row * share
    parents_share = lax.dynamic_slice_in_dim(parents, start, share, 0)
    tops_share = lax.dynamic_slice_in_dim(topall, start, share, 0)
    carried = batched(jnp.take(first_full, parents_share, axis=0), tops_share)
    base_terms = batched(chosen_two, lowsec)
    updated = lax.dynamic_slice_in_dim(base_terms, start, share, 0) + carried
    second_terms = lax.dynamic_update_slice_in_dim(base_terms, updated, start, 0)
    second_full = -lax.psum(second_terms, "prow")
    rows_one, valid_one = pick_rows(owned_slot_list == my_col, total_one // per_row_anc)
    pivot_small = valid_one * batched_left_t(
        jnp.take(lowall, rows_one, axis=0), jnp.take(first_full, rows_one, axis=0)
    )
    pivot_terms = jnp.zeros_like(first_full).at[rows_one].add(pivot_small)
    pivot_part = lax.psum_scatter(pivot_terms, "pcol", scatter_dimension=0, tiled=True)
    pivot_sum = over_copies(pivot_part, "prow")
    diag_one = pivot_one - pivot_sum
    count_one = first_full.shape[0] // row_count
    column_one = lax.dynamic_slice_in_dim(first_full, my_row * count_one, count_one, 0)
    second_level_count = second_full.shape[0] // row_count
    column_two = lax.dynamic_slice_in_dim(
        second_full, my_row * second_level_count, second_level_count, 0
    )
    rows_two, valid_two = pick_rows(my_slots_two == my_col, total_two // per_row_anc)
    lows_picked = jnp.take(lowsec, rows_two, axis=0)
    parent_picked = jnp.take(first_full, jnp.take(parents, rows_two, axis=0), axis=0)
    cross_small = valid_two * batched_left_t(parent_picked, lows_picked)
    diag_small = valid_two * batched_left_t(lows_picked, jnp.take(second_full, rows_two, axis=0))
    local_parent = parents - my_col * per_col_one
    own_parent = (local_parent >= 0) & (local_parent < per_col_one)
    rows_own, valid_own = pick_rows(own_parent, per_col_two)
    valid_own = valid_own * (my_row == 0).astype(jnp.float32)
    local_picked = jnp.clip(jnp.take(local_parent, rows_own, axis=0), 0, per_col_one - 1)
    picked = jnp.take(diag_one, local_picked, axis=0)
    own_small = valid_own * batched(picked, jnp.take(topall, rows_own, axis=0))
    cross_terms = (
        jnp.zeros_like(second_full).at[rows_two].add(cross_small).at[rows_own].add(own_small)
    )
    diag_terms = jnp.zeros_like(second_full).at[rows_two].add(diag_small)
    part_cross, part_diag = side_by_side((cross_terms, diag_terms), "pcol", 0, 1)
    sum_cross, sum_diag = together((part_cross, part_diag), "prow")
    second_parent_inverse = -sum_cross
    second_diagonal_inverse = (
        second_pivot_inverse
        - batched_left_t(second_scaled_factor, second_parent_inverse)
        - sum_diag
    )
    return (column_one, diag_one, column_two, second_parent_inverse, second_diagonal_inverse)


def solution(mesh):
    placed = (
        P("pcol", "prow"),
        P(),
        P(),
        P("pcol", "prow", None),
        P("pcol", None, None),
        P("pcol", "prow", None),
        P("pcol", None, None),
        P("pcol", None, None),
    )
    return jax.shard_map(
        body,
        mesh=mesh,
        in_specs=placed,
        out_specs=(
            P("prow", "pcol", None),
            P("pcol", None, None),
            P("prow", "pcol", None),
            P("pcol", None, None),
            P("pcol", None, None),
        ),
        check_vma=False,
    )
```

profile of v0, /device:TPU:1, one launch (start us, length us, event | category | flops | bytes accessed | tf_op | source)
XLA Modules:
  0.0 673.7 jit_solution(4868192869001686954)
XLA Ops:
  7.2 0.7 all-gather.3.cloned.1.call-update
  7.9 1.2 copy.59
  9.2 0.2 copy.60
  9.4 0.8 copy.58
  10.3 0.7 compare_and_fusion.5
  11.0 2.8 gather_fusion.3
  13.8 56.2 %all-gather.3.cloned.1.call-done = f32[16,256,256]{2,1,0:T(8,128)} async-done(((f32[1,256,256]{2,1,0:T(8,128)}), f32[16,256,256]{2,1,0:T(8,128)}) %all-gather.3.cloned.1.call-update) | async-done | bytes 4194320 | tf_op jit(solution)/shard_map/all_gather | solution.py:79
  70.0 9.7 %fusion.2 = f32[16,256,256]{2,1,0:T(8,128)} fusion(f32[16,256,256]{2,1,0:T(8,128)} %all-gather.3.cloned.1.call-done, f32[16,256,256]{2,1,0:T(8,128)} %gather_fusion.3, pred[16]{0:T(512)(128)(4,1)S(1)} %compare_and_fusion.4), kind=kOutput, calls=%fused_computation.18 | convolution fusion | flops 3222274048 | bytes 12582928 | tf_op jit(solution)/shard_map/kab,kbd->kad/dot_general | solution.py:42
  79.8 0.9 copy-done.6
  80.8 0.8 pad_maximum_fusion.1
  81.9 1.2 sort.45
  83.1 0.6 gather_fusion.4
  83.8 4.2 gather_fusion.5
  88.0 95.9 %all-reduce.3.cloned.1.call-done = f32[16,256,256]{2,1,0:T(8,128)} async-done(((f32[16,256,256]{2,1,0:T(8,128)}), f32[16,256,256]{2,1,0:T(8,128)}) %all-reduce.3.cloned.1.call-update) | async-done | bytes 4194320 | tf_op jit(solution)/shard_map/psum | solution.py:89
  183.9 4.5 neg.15
  188.4 4.2 gather_fusion.6
  192.6 6.1 fusion.17
  198.7 2.4 broadcast.189.clone
  201.1 4.4 scatter_fusion
  205.5 0.5 all-reduce.5.cloned.1.call-start
  206.0 0.6 gather_fusion
  207.0 2.7 gather_fusion.7
  209.8 2.8 gather_fusion.1
  212.6 46.1 %all-gather.5.cloned.1.call-done = f32[16,512,256]{2,1,0:T(8,128)} async-done(((f32[1,512,256]{2,1,0:T(8,128)}), f32[16,512,256]{2,1,0:T(8,128)}) %all-gather.5.cloned.1.call-update) | async-done | bytes 8388624 | tf_op jit(solution)/shard_map/all_gather | solution.py:10
  258.7 6.4 fusion.67
  265.1 0.8 copy-done.1
  265.9 1.3 copy-done.2
  267.2 5.6 fusion
  272.9 2.5 fusion.32
  275.4 63.5 %reduce-scatter.3.cloned.1.call-done = f32[1,256,256]{2,1,0:T(8,128)} async-done(((f32[16,256,256]{2,1,0:T(8,128)}), f32[1,256,256]{2,1,0:T(8,128)}) %reduce-scatter.3.cloned.1.call-update) | async-done | bytes 262160 | tf_op jit(solution)/shard_map/reduce_scatter | solution.py:104
  339.0 2.5 broadcast_in_dim.110
  341.5 4.4 all-to-all-start
  345.9 1.2 sort.46
  347.2 0.6 gather_fusion.2
  347.8 0.6 gather_fusion.8
  348.5 1.2 sort.47
  349.9 0.6 dynamic-slice.18
  350.5 0.6 dynamic-slice.17
  352.3 0.7 and_reduce_fusion
  353.0 4.2 gather_fusion.9
  357.2 2.9 gather_fusion.10
  360.1 6.7 %fusion.22 = f32[8,256,256]{2,1,0:T(8,128)} fusion(f32[8,256,256]{2,1,0:T(8,128)S(1)} %gather_fusion.10, f32[8,256,256]{2,1,0:T(8,128)} %gather_fusion.9, f32[8]{0:T(128)S(1)} %get-tuple-element.106, pred[8]{0:T(512)(128)(4,1)S(1)} %get-tuple-element.93, pred[8]{0:T(512)(128)(4,1)S(1)} %get-tuple-element.91), kind=kOutput, calls=%fused_computation.34 | convolution fusion | flops 1612185600 | bytes 6291504 | tf_op jit(solution)/shard_map/kba,kbd->kad/dot_general | solution.py:46
  366.9 2.4 broadcast.189.clone.2
  369.3 5.3 scatter_fusion.1
  374.6 90.7 %all-reduce.5.cloned.1.call-done = f32[16,256,256]{2,1,0:T(8,128)} async-done(((f32[16,256,256]{2,1,0:T(8,128)}), f32[16,256,256]{2,1,0:T(8,128)}) %all-reduce.5.cloned.1.call-update) | async-done | bytes 4194320 | tf_op jit(solution)/shard_map/psum | solution.py:98
  465.3 4.5 neg.16
  469.7 4.2 gather_fusion.11
  474.0 6.7 fusion.27
  480.7 2.4 broadcast.189.clone.1
  483.0 4.4 scatter_fusion.2
  487.4 1.8 reduce_sum.20
  489.2 2.8 fusion.36
  492.0 7.4 %pad_maximum_fusion = f32[16,512,256]{2,1,0:T(8,128)} fusion(f32[16,256,256]{2,1,0:T(8,128)} %scatter_fusion.2, f32[16,256,256]{2,1,0:T(8,128)} %fusion.36), kind=kLoop, calls=%fused_computation.15 | loop fusion | flops 2097152 | bytes 16777216 | tf_op jit(solution)/shard_map/concatenate | solution.py:24
  499.5 100.2 %reduce-scatter.5.cloned.1.call-done = f32[1,512,256]{2,1,0:T(8,128)} async-done(((f32[16,512,256]{2,1,0:T(8,128)}), f32[1,512,256]{2,1,0:T(8,128)}) %reduce-scatter.5.cloned.1.call-update) | async-done | bytes 524304 | tf_op jit(solution)/shard_map/reduce_scatter | solution.py:25
  599.7 1.1 slice_bitcast_fusion.1
  601.1 4.1 broadcast_in_dim.125
  605.2 4.9 all-to-all-start.1
  610.3 1.9 constant_dynamic-slice_fusion.1
  612.1 1.9 constant_dynamic-slice_fusion
  614.0 44.8 %all-to-all-done.1 = f32[8,1,131072]{2,1,0:T(1,128)} async-done(((f32[8,1,131072]{2,1,0:T(1,128)}), f32[8,1,131072]{2,1,0:T(1,128)}, u32[]{:S(2)}, u32[]{:S(2)}) %all-to-all-start.1) | async-done | bytes 4194336 | tf_op jit(solution)/shard_map/all_to_all | solution.py:16
  658.8 5.2 reduce_sum.22
  664.1 0.8 neg.18
  665.1 0.6 fusion.38
  665.7 0.8 copy.68
  (64 shorter events, 2.1 us)
Async XLA Ops:
  7.2 62.9 %all-gather.3.cloned.1.call-start = ((), (), s32[]{:S(2)}) async-start(), calls=%async_computation.4 | async-start | bytes 4456448 | tf_op jit(solution)/shard_map/all_gather | solution.py:79
  7.9 176.0 %all-reduce.3.cloned.1.call-start = ((), (), s32[]{:S(2)}) async-start(), calls=%async_computation.5 | async-start | bytes 8388608 | tf_op jit(solution)/shard_map/psum | solution.py:89
  79.7 0.9 copy-start.6
  79.7 1.0 copy-start.9
  79.8 178.9 %all-gather.5.cloned.1.call-start = ((), (), s32[]{:S(2)}) async-start(), calls=%async_computation.7 | async-start | bytes 8912896 | tf_op jit(solution)/shard_map/all_gather | solution.py:10
  81.6 257.4 %reduce-scatter.3.cloned.1.call-start = ((), (), s32[]{:S(2)}) async-start(), calls=%async_computation.6 | async-start | bytes 4456448 | tf_op jit(solution)/shard_map/reduce_scatter | solution.py:104
  201.1 4.9 copy-start
  205.5 259.8 %all-reduce.5.cloned.1.call-start = ((), (), s32[]{:S(2)}) async-start(), calls=%async_computation.8 | async-start | bytes 8388608 | tf_op jit(solution)/shard_map/psum | solution.py:98
  258.7 7.2 %copy-start.1 = (f32[16,512,256]{2,1,0:T(8,128)S(1)}, f32[16,512,256]{2,1,0:T(8,128)}, u32[]{:S(2)}) copy-start(f32[16,512,256]{2,1,0:T(8,128)} %all-gather.5.cloned.1.call-done) | copy-start | bytes 25165828
  258.7 8.5 %copy-start.2 = (f32[16,256,256]{2,1,0:T(8,128)S(1)}, f32[16,256,256]{2,1,0:T(8,128)}, u32[]{:S(2)}) copy-start(f32[16,256,256]{2,1,0:T(8,128)} %gather_fusion.7) | copy-start | bytes 12582916
  267.2 5.6 copy-start.4
  275.4 76.9 %copy-start.10 = (s32[3]{0:T(128)S(1)}, s32[3]{0:T(128)}, u32[]{:S(2)}) copy-start(s32[3]{0:T(128)} %constant.173.clone.1) | copy-start | bytes 40
  341.5 145.9 %all-to-all-start = ((f32[8,1,256,256]{3,2,1,0:T(8,128)}), f32[8,1,256,256]{3,2,1,0:T(8,128)}, u32[]{:S(2)}, u32[]{:S(2)}) async-start(f32[8,1,256,256]{3,2,1,0:T(8,128)} %broadcast_in_dim.110), calls=%async_computation.1 | async-start | bytes 4194304 | tf_op jit(solution)/shard_map/all_to_all | solution.py:16
  345.9 253.8 %reduce-scatter.5.cloned.1.call-start = ((), (), s32[]{:S(2)}) async-start(), calls=%async_computation.9 | async-start | bytes 8912896 | tf_op jit(solution)/shard_map/reduce_scatter | solution.py:25
  480.7 2.4 copy-start.3
  483.0 6.1 copy-start.7
  489.2 10.2 %copy-start.5 = (f32[1,256,256]{2,1,0:T(8,128)}, f32[1,256,256]{2,1,0:T(8,128)S(1)}, u32[]{:S(2)}) copy-start(f32[1,256,256]{2,1,0:T(8,128)S(1)} %bitcast_subtract_fusion) | copy-start | bytes 786436
  605.2 4.9 copy-start.8
  605.2 53.5 %all-to-all-start.1 = ((f32[8,1,131072]{2,1,0:T(1,128)}), f32[8,1,131072]{2,1,0:T(1,128)}, u32[]{:S(2)}, u32[]{:S(2)}) async-start(f32[8,1,131072]{2,1,0:T(1,128)} %broadcast_in_dim.125), calls=%async_computation.3 | async-start | bytes 8388608 | tf_op jit(solution)/shard_map/all_to_all | solution.py:16
Sparse Core Ops, SparseCore 0:
  10.4 59.5 all-gather.2
  79.9 103.9 all-reduce.2
  186.9 71.8 all-gather.4
  262.6 76.3 reduce-scatter.2
  341.5 123.7 all-reduce.4
  499.6 100.0 reduce-scatter.4
where the time goes:
time: 683 us; the launch traced here: 674 us
  waiting for transfers between devices  498 us (73%)
  local copies, waits for them, and re-layouts  64.3 us (9%)
  other arithmetic  44.5 us (7%)
  matrix products  40.7 us (6%)
  between operations  16 us (2%)
  starting transfers between devices  9.97 us (1%)
    reduce_scatter x1, waiting for transfers between devices, side_by_side(): lax.psum_scatter(both, axis, scatter_dimension=dim, tiled=True)  100 us
    psum x1, waiting for transfers between devices, body(): first_full = -lax.psum(first_terms, 'prow')  95.9 us
    psum x1, waiting for transfers between devices, body(): second_full = -lax.psum(second_terms, 'prow')  90.7 us
    reduce_scatter x1, waiting for transfers between devices, body(): lax.psum_scatter(pivot_terms, 'pcol', scatter_dimension=0, tiled=True)  63.5 us
    all_gather x1, waiting for transfers between devices, body(): lowall = lax.all_gather(low_one, 'pcol', axis=0, tiled=True)  56.2 us
    all_gather x1, waiting for transfers between devices, in_one_piece(): result = lax.all_gather(both, axis, axis=dim, tiled=True)  46.1 us
    all_to_all x2, waiting for transfers between devices, sent_to_all(): return lax.all_to_all(copies, axis, split_axis=0, concat_axis=0, tiled=True)  44.8 us
    dot_general x4, matrix products, batched(): jnp.einsum('kab,kbd->kad', left, right, precision=lax.Precision.HIGHEST)  20.6 us
  transfers between devices with their start and end apart: 8, of which 7 were waited for; matrix products, arithmetic and copies ran while one was open for 17% of the time, Pallas kernels for 0%

commit v1 on v0

--- a/solution.py
+++ b/solution.py
@@ -76,7 +76,9 @@
     zblocks = anc_inverse.reshape(supernode_block_width, owned, supernode_block_width).transpose(
         1, 0, 2
     )
-    lowall = lax.all_gather(low_one, "pcol", axis=0, tiled=True)
+    lowall = jnp.concatenate(
+        lax.all_to_all(jnp.stack([low_one] * lax.axis_size("pcol")), "pcol", 0, 0), axis=0
+    )
     total_one = lowall.shape[0]
     owned_slot_list = lax.dynamic_index_in_dim(pattern_one, my_row, 1, keepdims=False)
     chosen = jnp.take(zblocks, owned_slot_list - my_row * owned, axis=0)

time: 683 us -> 614 us (0.90)
  waiting for transfers between devices: 498 us -> 407 us
  starting transfers between devices: 9.97 us -> 33.1 us
    psum x1, waiting for transfers between devices: 90.7 us -> 23.9 us  [body(): second_full = -lax.psum(second_terms, 'prow')]
    all_gather x1 -> x0, waiting for transfers between devices: 56.2 us -> none  [body(): lowall = lax.all_gather(low_one, 'pcol', axis=0, tiled=True)]
    all_to_all x0 -> x1, waiting for transfers between devices: none -> 49.2 us  [body(): lax.all_to_all(jnp.stack([low_one] * lax.axis_size('pcol')), 'pcol', 0, 0)]
    all_gather x1, waiting for transfers between devices: 46.1 us -> 0.03 us  [in_one_piece(): result = lax.all_gather(both, axis, axis=dim, tiled=True)]
    psum x1, waiting for transfers between devices: 95.9 us -> 133 us  [body(): first_full = -lax.psum(first_terms, 'prow')]
    reduce_scatter x1, starting transfers between devices: 0.04 us -> 10.9 us  [side_by_side(): lax.psum_scatter(both, axis, scatter_dimension=dim, tiled=True)]
    all_to_all x0 -> x1, starting transfers between devices: none -> 8.58 us  [body(): lax.all_to_all(jnp.stack([low_one] * lax.axis_size('pcol')), 'pcol', 0, 0)]
  transfers between devices with their start and end apart: 8 -> 8, of which waited for: 7 -> 7; matrix products, arithmetic and copies ran while one was open for 17% -> 15% of each run, Pallas kernels for 0% -> 0%
where the time goes in v1:
time: 614 us; the launch traced here: 609 us
  waiting for transfers between devices  407 us (66%)
  local copies, waits for them, and re-layouts  66.8 us (11%)
  other arithmetic  43.6 us (7%)
  matrix products  40.8 us (7%)
  starting transfers between devices  33.1 us (5%)
  between operations  17.6 us (3%)
    psum x1, waiting for transfers between devices, body(): first_full = -lax.psum(first_terms, 'prow')  133 us
    reduce_scatter x1, waiting for transfers between devices, side_by_side(): lax.psum_scatter(both, axis, scatter_dimension=dim, tiled=True)  97.9 us
    reduce_scatter x1, waiting for transfers between devices, body(): lax.psum_scatter(pivot_terms, 'pcol', scatter_dimension=0, tiled=True)  57.6 us
    all_to_all x1, waiting for transfers between devices, body(): lax.all_to_all(jnp.stack([low_one] * lax.axis_size('pcol')), 'pcol', 0, 0)  49.2 us
    all_to_all x2, waiting for transfers between devices, sent_to_all(): return lax.all_to_all(copies, axis, split_axis=0, concat_axis=0, tiled=True)  45.2 us
    psum x1, waiting for transfers between devices, body(): second_full = -lax.psum(second_terms, 'prow')  23.9 us
    dot_general x4, matrix products, batched(): jnp.einsum('kab,kbd->kad', left, right, precision=lax.Precision.HIGHEST)  20.6 us
    dot_general x4, matrix products, batched_left_t(): jnp.einsum('kba,kbd->kad', left, right, precision=lax.Precision.HIGHEST)  20.2 us
  transfers between devices with their start and end apart: 8, of which 7 were waited for; matrix products, arithmetic and copies ran while one was open for 15% of the time, Pallas kernels for 0%

profile of v1, /device:TPU:1, one launch (start us, length us, event | category | flops | bytes accessed | tf_op | source)
XLA Modules:
  0.0 608.6 jit_solution(18038225165876086862)
XLA Ops:
  8.0 3.3 stack.2
  11.3 8.6 %all-to-all-start = ((f32[16,1,256,256]{3,2,1,0:T(8,128)}), f32[16,1,256,256]{3,2,1,0:T(8,128)}, u32[]{:S(2)}, u32[]{:S(2)}) async-start(f32[16,1,256,256]{3,2,1,0:T(8,128)} %stack.2), calls=%async_computation | async-start | bytes 8388608 | tf_op jit(solution)/shard_map/all_to_all | solution.py:80
  20.0 0.2 copy.59
  20.2 0.2 copy.60
  20.6 2.8 gather_fusion.3
  23.4 49.2 %all-to-all-done = f32[16,1,256,256]{3,2,1,0:T(8,128)} async-done(((f32[16,1,256,256]{3,2,1,0:T(8,128)}), f32[16,1,256,256]{3,2,1,0:T(8,128)}, u32[]{:S(2)}, u32[]{:S(2)}) %all-to-all-start) | async-done | bytes 4194336 | tf_op jit(solution)/shard_map/all_to_all | solution.py:80
  72.6 9.7 %fusion.2 = f32[16,256,256]{2,1,0:T(8,128)} fusion(f32[16,256,256]{2,1,0:T(8,128)} %gather_fusion.3, pred[16]{0:T(512)(128)(4,1)S(1)} %compare_and_fusion.4, f32[16,1,256,256]{3,2,1,0:T(8,128)} %all-to-all-done), kind=kOutput, calls=%fused_computation.18 | convolution fusion | flops 3222274048 | bytes 12582928 | tf_op jit(solution)/shard_map/kab,kbd->kad/dot_general | solution.py:42
  82.4 0.9 copy-done.6
  83.3 0.8 pad_maximum_fusion.1
  84.2 0.4 reduce-scatter.3.cloned.1.call-start
  84.8 1.2 sort.45
  86.1 0.6 gather_fusion.4
  86.7 4.2 gather_fusion.5
  90.9 132.7 %all-reduce.3.cloned.1.call-done = f32[16,256,256]{2,1,0:T(8,128)} async-done(((f32[16,256,256]{2,1,0:T(8,128)}), f32[16,256,256]{2,1,0:T(8,128)}) %all-reduce.3.cloned.1.call-update) | async-done | bytes 4194320 | tf_op jit(solution)/shard_map/psum | solution.py:91
  223.6 4.5 neg.15
  228.1 4.2 gather_fusion.6
  232.3 6.1 fusion.17
  238.4 2.4 broadcast.192.clone
  240.8 4.4 scatter_fusion
  245.3 0.6 gather_fusion
  246.3 2.7 gather_fusion.7
  249.1 2.8 gather_fusion.1
  251.9 6.8 %fusion.68 = (f32[16,256,256]{2,1,0:T(8,128)}, f32[16,256,256]{2,1,0:T(8,128)S(1)}) fusion(f32[16,512,256]{2,1,0:T(8,128)} %all-gather.2.cloned.1.call-done), kind=kLoop, calls=%fused_computation.118 | loop fusion | bytes 16777216 | tf_op jit(solution)/shard_map/split | solution.py:11
  258.7 1.2 copy-done.1
  259.9 1.4 copy-done.2
  261.3 5.6 fusion
  267.0 2.5 fusion.32
  269.5 57.6 %reduce-scatter.3.cloned.1.call-done = f32[1,256,256]{2,1,0:T(8,128)} async-done(((f32[16,256,256]{2,1,0:T(8,128)}), f32[1,256,256]{2,1,0:T(8,128)}) %reduce-scatter.3.cloned.1.call-update) | async-done | bytes 262160 | tf_op jit(solution)/shard_map/reduce_scatter | solution.py:106
  327.2 2.5 broadcast_in_dim.110
  329.7 8.3 %all-to-all-start.1 = ((f32[8,1,256,256]{3,2,1,0:T(8,128)}), f32[8,1,256,256]{3,2,1,0:T(8,128)}, u32[]{:S(2)}, u32[]{:S(2)}) async-start(f32[8,1,256,256]{3,2,1,0:T(8,128)} %broadcast_in_dim.110), calls=%async_computation.2 | async-start | bytes 4194304 | tf_op jit(solution)/shard_map/all_to_all | solution.py:16
  337.9 10.9 %reduce-scatter.5.cloned.1.call-start = ((), (), s32[]{:S(2)}) async-start(), calls=%async_computation.9 | async-start | bytes 8912896 | tf_op jit(solution)/shard_map/reduce_scatter | solution.py:25
  348.8 1.2 sort.46
  350.1 0.6 gather_fusion.8
  350.7 0.6 gather_fusion.2
  351.4 1.3 sort.47
  352.8 0.6 dynamic-slice.18
  353.3 0.6 dynamic-slice.17
  355.2 0.7 and_reduce_fusion
  355.9 4.2 gather_fusion.9
  360.1 2.9 gather_fusion.10
  363.0 6.8 %fusion.22 = f32[8,256,256]{2,1,0:T(8,128)} fusion(f32[8,256,256]{2,1,0:T(8,128)S(1)} %gather_fusion.10, f32[8,256,256]{2,1,0:T(8,128)} %gather_fusion.9, f32[8]{0:T(128)S(1)} %get-tuple-element.106, pred[8]{0:T(512)(128)(4,1)S(1)} %get-tuple-element.93, pred[8]{0:T(512)(128)(4,1)S(1)} %get-tuple-element.91), kind=kOutput, calls=%fused_computation.34 | convolution fusion | flops 1612185600 | bytes 6291504 | tf_op jit(solution)/shard_map/kba,kbd->kad/dot_general | solution.py:46
  369.8 2.4 broadcast.192.clone.2
  372.2 5.1 scatter_fusion.1
  377.3 0.3 all-to-all-done.1
  377.6 1.8 reduce_sum.20
  379.5 2.8 fusion.36
  382.2 23.9 %all-reduce.5.cloned.1.call-done = f32[16,256,256]{2,1,0:T(8,128)} async-done(((f32[16,256,256]{2,1,0:T(8,128)}), f32[16,256,256]{2,1,0:T(8,128)}) %all-reduce.5.cloned.1.call-update) | async-done | bytes 4194320 | tf_op jit(solution)/shard_map/psum | solution.py:100
  406.1 4.5 neg.16
  410.6 4.2 gather_fusion.11
  414.8 6.8 %fusion.27 = f32[8,256,256]{2,1,0:T(8,128)} fusion(f32[8,256,256]{2,1,0:T(8,128)} %gather_fusion.11, f32[8,256,256]{2,1,0:T(8,128)S(1)} %gather_fusion.10, f32[8]{0:T(128)S(1)} %get-tuple-element.106, pred[8]{0:T(512)(128)(4,1)S(1)} %get-tuple-element.93), kind=kOutput, calls=%fused_computation.35 | convolution fusion | flops 1612185600 | bytes 6291496 | tf_op jit(solution)/shard_map/kba,kbd->kad/dot_general | solution.py:46
  421.6 2.4 broadcast.192.clone.1
  424.0 4.4 scatter_fusion.2
  428.3 7.4 %pad_maximum_fusion = f32[16,512,256]{2,1,0:T(8,128)} fusion(f32[16,256,256]{2,1,0:T(8,128)} %scatter_fusion.2, f32[16,256,256]{2,1,0:T(8,128)} %fusion.36), kind=kLoop, calls=%fused_computation.15 | loop fusion | flops 2097152 | bytes 16777216 | tf_op jit(solution)/shard_map/concatenate | solution.py:24
  435.8 97.9 %reduce-scatter.5.cloned.1.call-done = f32[1,512,256]{2,1,0:T(8,128)} async-done(((f32[16,512,256]{2,1,0:T(8,128)}), f32[1,512,256]{2,1,0:T(8,128)}) %reduce-scatter.5.cloned.1.call-update) | async-done | bytes 524304 | tf_op jit(solution)/shard_map/reduce_scatter | solution.py:25
  533.7 1.1 slice_bitcast_fusion.1
  535.1 4.1 broadcast_in_dim.125
  539.2 4.9 all-to-all-start.2
  544.2 1.9 constant_dynamic-slice_fusion.1
  546.1 1.9 constant_dynamic-slice_fusion
  548.0 44.9 %all-to-all-done.2 = f32[8,1,131072]{2,1,0:T(1,128)} async-done(((f32[8,1,131072]{2,1,0:T(1,128)}), f32[8,1,131072]{2,1,0:T(1,128)}, u32[]{:S(2)}, u32[]{:S(2)}) %all-to-all-start.2) | async-done | bytes 4194336 | tf_op jit(solution)/shard_map/all_to_all | solution.py:16
  592.9 5.3 reduce_sum.22
  598.3 0.8 neg.18
  599.3 0.6 fusion.38
  599.9 0.8 copy.68
  (68 shorter events, 2.2 us)
Async XLA Ops:
  11.3 8.6 %copy-start.11 = (s32[16,8]{0,1:T(8,128)S(1)}, s32[16,8]{0,1:T(8,128)}, u32[]{:S(2)}) copy-start(s32[16,8]{0,1:T(8,128)} %param.17) | copy-start | bytes 1540
  11.3 8.7 %copy-start.7 = (f32[256,512]{1,0:T(8,128)S(1)}, f32[256,512]{1,0:T(8,128)}, u32[]{:S(2)}) copy-start(f32[256,512]{1,0:T(8,128)} %param.16) | copy-start | bytes 1572868
  11.3 9.3 %copy-start = (s32[16]{0:T(128)S(1)}, s32[16]{0:T(128)}, u32[]{:S(2)}) copy-start(s32[16]{0:T(128)} %param.18) | copy-start | bytes 196
  11.3 61.3 %all-to-all-start = ((f32[16,1,256,256]{3,2,1,0:T(8,128)}), f32[16,1,256,256]{3,2,1,0:T(8,128)}, u32[]{:S(2)}, u32[]{:S(2)}) async-start(f32[16,1,256,256]{3,2,1,0:T(8,128)} %stack.2), calls=%async_computation | async-start | bytes 8388608 | tf_op jit(solution)/shard_map/all_to_all | solution.py:80
  19.9 203.7 %all-reduce.3.cloned.1.call-start = ((), (), s32[]{:S(2)}) async-start(), calls=%async_computation.5 | async-start | bytes 8388608 | tf_op jit(solution)/shard_map/psum | solution.py:91
  82.3 0.9 copy-start.6
  82.3 1.0 copy-start.10
  82.3 169.6 %all-gather.2.cloned.1.call-start = ((), (), s32[]{:S(2)}) async-start(), calls=%async_computation.7 | async-start | bytes 8912896 | tf_op jit(solution)/shard_map/all_gather | solution.py:10
  84.2 243.0 %reduce-scatter.3.cloned.1.call-start = ((), (), s32[]{:S(2)}) async-start(), calls=%async_computation.6 | async-start | bytes 4456448 | tf_op jit(solution)/shard_map/reduce_scatter | solution.py:106
  245.2 160.9 %all-reduce.5.cloned.1.call-start = ((), (), s32[]{:S(2)}) async-start(), calls=%async_computation.8 | async-start | bytes 8388608 | tf_op jit(solution)/shard_map/psum | solution.py:100
  251.9 8.0 %copy-start.1 = (f32[16,512,256]{2,1,0:T(8,128)S(1)}, f32[16,512,256]{2,1,0:T(8,128)}, u32[]{:S(2)}) copy-start(f32[16,512,256]{2,1,0:T(8,128)} %all-gather.2.cloned.1.call-done) | copy-start | bytes 25165828
  251.9 9.4 %copy-start.2 = (f32[16,256,256]{2,1,0:T(8,128)S(1)}, f32[16,256,256]{2,1,0:T(8,128)}, u32[]{:S(2)}) copy-start(f32[16,256,256]{2,1,0:T(8,128)} %gather_fusion.7) | copy-start | bytes 12582916
  261.3 5.6 copy-start.4
  269.5 85.7 %copy-start.12 = (s32[3]{0:T(128)S(1)}, s32[3]{0:T(128)}, u32[]{:S(2)}) copy-start(s32[3]{0:T(128)} %constant.173.clone.1) | copy-start | bytes 40
  329.7 47.9 %all-to-all-start.1 = ((f32[8,1,256,256]{3,2,1,0:T(8,128)}), f32[8,1,256,256]{3,2,1,0:T(8,128)}, u32[]{:S(2)}, u32[]{:S(2)}) async-start(f32[8,1,256,256]{3,2,1,0:T(8,128)} %broadcast_in_dim.110), calls=%async_computation.2 | async-start | bytes 4194304 | tf_op jit(solution)/shard_map/all_to_all | solution.py:16
  337.9 195.7 %reduce-scatter.5.cloned.1.call-start = ((), (), s32[]{:S(2)}) async-start(), calls=%async_computation.9 | async-start | bytes 8912896 | tf_op jit(solution)/shard_map/reduce_scatter | solution.py:25
  372.2 7.2 %copy-start.8 = (f32[1,256,256]{2,1,0:T(8,128)S(1)}, f32[1,256,256]{2,1,0:T(8,128)}, u32[]{:S(2)}) copy-start(f32[1,256,256]{2,1,0:T(8,128)} %param.20) | copy-start | bytes 786436
  379.4 31.2 %copy-start.5 = (f32[1,256,256]{2,1,0:T(8,128)}, f32[1,256,256]{2,1,0:T(8,128)S(1)}, u32[]{:S(2)}) copy-start(f32[1,256,256]{2,1,0:T(8,128)S(1)} %bitcast_subtract_fusion) | copy-start | bytes 786436
  421.6 2.4 copy-start.3
  539.2 4.9 copy-start.9
  539.2 53.7 %all-to-all-start.2 = ((f32[8,1,131072]{2,1,0:T(1,128)}), f32[8,1,131072]{2,1,0:T(1,128)}, u32[]{:S(2)}, u32[]{:S(2)}) async-start(f32[8,1,131072]{2,1,0:T(1,128)} %broadcast_in_dim.125), calls=%async_computation.4 | async-start | bytes 8388608 | tf_op jit(solution)/shard_map/all_to_all | solution.py:16
Sparse Core Ops, SparseCore 0:
  82.4 141.1 all-reduce.2
  269.6 136.4 all-reduce.4
Sparse Core Ops, SparseCore 1:
  85.8 84.5 all-gather.1
  245.3 81.8 reduce-scatter.2
  435.9 97.8 reduce-scatter.4
